TPU v7x, 512 devices: a whole 4x4x16 slice. The times are simulated.
512 devices in a mesh: dp: 32 (over z_lo, x), tensor: 16 (over z_hi, y, core).
Axes of the slice: x: 4, y: 4, z: 16 (z_hi: 2, z_lo: 8; z = z_hi * 8 + z_lo), core: 2. Of those that a mesh axis runs over, the one named last changes fastest.
Arguments:
- out_grad: bfloat16 [4096, 4096], P(('dp', 'tensor')), may hold values from -6 to 6
- gate_pre: bfloat16 [4096, 14336], P('dp', 'tensor'), may hold values from -6 to 6
- up_pre: bfloat16 [4096, 14336], P('dp', 'tensor'), may hold values from -6 to 6
- down_weight: bfloat16 [14336, 4096], P('tensor', 'dp'), may hold values from -6 to 6
- moment: float32 [14336, 4096], P('tensor', 'dp'), may hold values from -4 to 4
- second: float32 [14336, 4096], P('tensor', 'dp'), may hold values from 0.01 to 0.5
- decay_mask: int32 [14336], P('tensor'), may hold values 0 or 1
Outputs:
- grad_gate: bfloat16 [4096, 14336], P('dp', 'tensor')
- grad_up: bfloat16 [4096, 14336], P('dp', 'tensor')
- new_weight: bfloat16 [14336, 4096], P('tensor', 'dp')
- new_moment: float32 [14336, 4096], P('tensor', 'dp')
- new_second: float32 [14336, 4096], P('tensor', 'dp')
All inputs are finite; a program needn't handle non-finite values. No bound on the sum of `decay_mask` on one device may be relied on, other than what follows from the above.
Results may differ from a plain program's by a relative error of at most 0.0014.
Values may be sent and summed in bfloat16 or wider, within the bound.
A program may use at most 64 MiB of HBM per device.

v0:
```python
import math
import jax
import jax.numpy as jnp
from jax import lax
from jax.sharding import Mesh
from jax.sharding import PartitionSpec as P

FF = 14336
OPT_STEP = 10
BETA_ONE = 0.9
BETA_TWO = 0.95
LEARN_RATE = 0.1
DECAY_RATE = 0.5
ADAM_EPS = 1e-08
DP = ("zl", "x")
TP = ("zh", "y", "c")


def body(out_grad, gate_pre, up_pre, down_weight, moment, second, decay_mask):
    factor = 1.0 / math.sqrt(FF)
    group_grad = lax.all_gather(out_grad, "c", axis=0, tiled=True)
    group_grad = lax.all_gather(group_grad, "y", axis=0, tiled=True)
    group_grad = lax.all_gather(group_grad, "zh", axis=0, tiled=True)
    gate = gate_pre.astype(jnp.float32)
    up = up_pre.astype(jnp.float32)
    sigmoid_gate = jax.nn.sigmoid(gate)
    activated = gate * sigmoid_gate
    hidden = (activated * up).astype(jnp.bfloat16)
    columns = lax.all_to_all(group_grad, DP, split_axis=1, concat_axis=0, tiled=True)
    stacked = jnp.stack([down_weight, hidden.T])
    stacked = lax.all_gather(stacked, "x", axis=2, tiled=True)
    stacked = lax.all_gather(stacked, "zl", axis=2, tiled=True)
    back_sum = lax.dot_general(
        group_grad, stacked[0], (((1,), (1,)), ((), ())), preferred_element_type=jnp.float32
    )
    grad_sum = lax.dot_general(
        stacked[1], columns, (((1,), (0,)), ((), ())), preferred_element_type=jnp.float32
    )
    back = back_sum * factor
    grad_up = (back * activated).astype(jnp.bfloat16)
    grad_gate = (back * up * sigmoid_gate * (1.0 + gate * (1.0 - sigmoid_gate))).astype(
        jnp.bfloat16
    )
    weight_grad = grad_sum * factor
    new_moment = BETA_ONE * moment + (1.0 - BETA_ONE) * weight_grad
    new_second = BETA_TWO * second + (1.0 - BETA_TWO) * weight_grad * weight_grad
    fix_one = 1.0 - BETA_ONE**OPT_STEP
    fix_two = 1.0 - BETA_TWO**OPT_STEP
    weight = down_weight.astype(jnp.float32)
    decay = decay_mask.astype(jnp.float32)[:, None]
    direction = (
        new_moment / fix_one / (jnp.sqrt(new_second / fix_two) + ADAM_EPS)
        + DECAY_RATE * decay * weight
    )
    new_weight = (weight - LEARN_RATE * direction).astype(jnp.bfloat16)
    return (grad_gate, grad_up, new_weight, new_moment, new_second)


def solution(mesh):
    zl, x = (8, mesh.shape["dp"] // 8)
    zh = mesh.shape["tensor"] // 8
    fine = Mesh(mesh.devices.reshape(zl, x, zh, 4, 2), DP + TP)
    return jax.shard_map(
        body,
        mesh=fine,
        in_specs=(P(DP + TP, None), P(DP, TP), P(DP, TP), P(TP, DP), P(TP, DP), P(TP, DP), P(TP)),
        out_specs=(P(DP, TP), P(DP, TP), P(TP, DP), P(TP, DP), P(TP, DP)),
        check_vma=False,
    )
```

profile of v0, /device:TPU:105, one launch (start us, length us, event | category | flops | bytes accessed | tf_op | source)
XLA Modules:
  0.0 484.9 jit_solution(10351806163342086163)
XLA Ops:
  7.2 0.0 all-gather.4.cloned.1.call-start
  7.2 1.1 copy.26
  8.3 1.1 copy.27
  9.4 0.1 fusion.15
  9.6 0.0 copy-start
  9.6 0.0 copy-start.1
  9.6 1.8 pad_maximum_fusion
  11.4 0.0 all-gather.4.cloned.1.call-update
  11.4 0.0 all-gather.8.cloned.1.call-start
  11.5 2.4 all_gather.17
  13.9 10.8 %all_gather.18 = bf16[64,4096]{1,0:T(8,128)(2,1)} all-gather(bf16[16,4096]{1,0:T(8,128)(2,1)S(1)} %all_gather.17), channel_id=1, replica_groups=mesh['zl'=8,'x'=4,'zh'=2,'y'=4,'c'=2] {'y'}, dimensions={0}, use_global_device_ids=true | all-gather | bytes 655360 | tf_op jit(solution)/shard_map/all_gather | solution.py:22
  24.8 0.0 all-gather.8.cloned.1.call-update
  24.8 0.0 all-gather.6.cloned.1.call-start
  24.9 29.2 %all-gather.4.cloned.1.call-done = bf16[2,896,512]{2,1,0:T(8,128)(2,1)} async-done(((bf16[2,896,128]{2,1,0:T(8,128)(2,1)}), bf16[2,896,512]{2,1,0:T(8,128)(2,1)}) %all-gather.4.cloned.1.call-update) | async-done | bytes 1835024 | tf_op jit(solution)/shard_map/all_gather | solution.py:31
  54.0 0.0 all-gather.6.cloned.1.call-update
  54.0 76.9 %all-gather.8.cloned.1.call-done = bf16[128,4096]{1,0:T(8,128)(2,1)} async-done(((bf16[64,4096]{1,0:T(8,128)(2,1)}), bf16[128,4096]{1,0:T(8,128)(2,1)}) %all-gather.8.cloned.1.call-update) | async-done | bytes 1048592 | tf_op jit(solution)/shard_map/all_gather | solution.py:23
  131.0 2.3 copy.28
  133.3 7.1 %all-to-all-start = ((bf16[128,32,128]{0,2,1:T(8,128)(2,1)}), bf16[128,32,128]{0,2,1:T(8,128)(2,1)S(1)}, u32[]{:S(2)}, u32[]{:S(2)}) async-start(bf16[128,32,128]{0,2,1:T(8,128)(2,1)} %bitcast.6), calls=%async_computation | async-start | bytes 2097152 | tf_op jit(solution)/shard_map/all_to_all | solution.py:29
  140.4 0.7 convert_multiply_fusion.5
  141.1 92.0 %all-to-all-done = bf16[128,32,128]{0,2,1:T(8,128)(2,1)S(1)} async-done(((bf16[128,32,128]{0,2,1:T(8,128)(2,1)}), bf16[128,32,128]{0,2,1:T(8,128)(2,1)S(1)}, u32[]{:S(2)}, u32[]{:S(2)}) %all-to-all-start) | async-done | bytes 1048608 | tf_op jit(solution)/shard_map/all_to_all | solution.py:29
  233.1 0.7 copy.29
  233.8 0.0 copy-start.2
  233.8 231.0 %all-gather.6.cloned.1.call-done = bf16[2,896,4096]{2,1,0:T(8,128)(2,1)} async-done(((bf16[2,896,512]{2,1,0:T(8,128)(2,1)}), bf16[2,896,4096]{2,1,0:T(8,128)(2,1)}) %all-gather.6.cloned.1.call-update) | async-done | bytes 14680080 | tf_op jit(solution)/shard_map/all_gather | solution.py:32
  464.9 5.4 %multiply_convert_fusion = (bf16[128,896]{0,1:T(8,128)(2,1)S(1)}, bf16[128,896]{0,1:T(8,128)(2,1)S(1)}) fusion(bf16[128,896]{0,1:T(8,128)(2,1)S(1)} %copy.26, bf16[128,896]{0,1:T(8,128)(2,1)S(1)} %copy.27, bf16[128,4096]{1,0:T(8,128)(2,1)} %all-gather.8.cloned.1.call-done, bf16[2,896,4096]{2,1,0:T(8,128)(2,1)} %all-gather.6.cloned.1.call-done), kind=kOutput, calls=%fused_computation.27 | convolution fusion | flops 941359104 | bytes 9306112 | tf_op jit(solution)/shard_map/dot_general | solution.py:33
  470.3 0.8 copy.31
  471.2 0.8 copy.30
  472.0 0.0 copy-done
  472.0 0.0 copy-done.1
  472.0 0.0 copy-done.2
  472.0 6.4 %fusion.10 = (bf16[896,128]{1,0:T(8,128)(2,1)}, f32[896,128]{1,0:T(8,128)}, f32[896,128]{1,0:T(8,128)}) fusion(bf16[896,128]{1,0:T(8,128)(2,1)S(1)} %copy-done, f32[896]{0:T(1024)S(1)} %convert_multiply_fusion.5, f32[896,128]{1,0:T(8,128)S(1)} %copy-done.1, f32[896,128]{1,0:T(8,128)S(1)} %copy-done.2, bf16[4096,128]{1,0:T(8,128)(2,1)S(1)} %bitcast.27, ...), kind=kOutput, calls=%fused_computation.19 | convolution fusion | flops 941588480 | bytes 10685952 | tf_op jit(solution)/shard_map/dot_general | solution.py:36
Async XLA Ops:
  7.2 46.8 %all-gather.4.cloned.1.call-start = ((), (), s32[]{:S(2)}) async-start(), calls=%async_computation.1 | async-start | bytes 2293760 | tf_op jit(solution)/shard_map/all_gather | solution.py:31
  9.6 462.4 %copy-start = (bf16[896,128]{1,0:T(8,128)(2,1)S(1)}, bf16[896,128]{1,0:T(8,128)(2,1)}, u32[]{:S(2)}) copy-start(bf16[896,128]{1,0:T(8,128)(2,1)} %param.10) | copy-start | bytes 688132
  9.6 462.4 %copy-start.1 = (f32[896,128]{1,0:T(8,128)S(1)}, f32[896,128]{1,0:T(8,128)}, u32[]{:S(2)}) copy-start(f32[896,128]{1,0:T(8,128)} %param.11) | copy-start | bytes 1376260
  11.4 119.5 %all-gather.8.cloned.1.call-start = ((), (), s32[]{:S(2)}) async-start(), calls=%async_computation.3 | async-start | bytes 1572864 | tf_op jit(solution)/shard_map/all_gather | solution.py:23
  24.8 440.1 %all-gather.6.cloned.1.call-start = ((), (), s32[]{:S(2)}) async-start(), calls=%async_computation.2 | async-start | bytes 16515072 | tf_op jit(solution)/shard_map/all_gather | solution.py:32
  133.3 99.9 %all-to-all-start = ((bf16[128,32,128]{0,2,1:T(8,128)(2,1)}), bf16[128,32,128]{0,2,1:T(8,128)(2,1)S(1)}, u32[]{:S(2)}, u32[]{:S(2)}) async-start(bf16[128,32,128]{0,2,1:T(8,128)(2,1)} %bitcast.6), calls=%async_computation | async-start | bytes 2097152 | tf_op jit(solution)/shard_map/all_to_all | solution.py:29
  233.8 238.2 %copy-start.2 = (f32[896,128]{1,0:T(8,128)S(1)}, f32[896,128]{1,0:T(8,128)}, u32[]{:S(2)}) copy-start(f32[896,128]{1,0:T(8,128)} %param.12) | copy-start | bytes 1376260
Sparse Core Ops, SparseCore 0:
  11.6 42.3 all-gather.3
  56.1 74.8 all-gather.7
  133.1 331.7 all-gather.5
where the time goes:
time: 485 us
  waiting for transfers between devices  429 us (88%)
  between operations  13.8 us (3%)
  blocking collectives  13.3 us (3%)
  matrix products  11.8 us (2%)
  starting transfers between devices  7.26 us (1%)
  local copies, waits for them, and re-layouts  6.87 us (1%)
    all_gather x1, waiting for transfers between devices, body(): stacked = lax.all_gather(stacked, 'zl', axis=2, tiled=True)  231 us
    all_to_all x1, waiting for transfers between devices, body(): lax.all_to_all(group_grad, DP, split_axis=1, concat_axis=0, tiled=True)  92 us
    all_gather x1, waiting for transfers between devices, body(): group_grad = lax.all_gather(group_grad, 'zh', axis=0, tiled=True)  76.9 us
    all_gather x1, waiting for transfers between devices, body(): stacked = lax.all_gather(stacked, 'x', axis=2, tiled=True)  29.2 us
    all_gather x1, blocking collectives, body(): group_grad = lax.all_gather(group_grad, 'y', axis=0, tiled=True)  10.8 us
  transfers between devices with their start and end apart: 4, of which 4 were waited for; matrix products, arithmetic and copies ran while one was open for 1% of the time, Pallas kernels for 0%

commit v1 on v0

--- a/solution.py
+++ b/solution.py
@@ -28,7 +28,9 @@
     hidden = (activated * up).astype(jnp.bfloat16)
     columns = lax.all_to_all(group_grad, DP, split_axis=1, concat_axis=0, tiled=True)
     stacked = jnp.stack([down_weight, hidden.T])
-    stacked = lax.all_gather(stacked, "x", axis=2, tiled=True)
+    stacked = jnp.concatenate(
+        lax.all_to_all(jnp.stack([stacked] * lax.axis_size("x")), "x", 0, 0), axis=2
+    )
     stacked = lax.all_gather(stacked, "zl", axis=2, tiled=True)
     back_sum = lax.dot_general(
         group_grad, stacked[0], (((1,), (1,)), ((), ())), preferred_element_type=jnp.float32

time: 485 us -> 464 us (0.957)
  waiting for transfers between devices: 429 us -> 401 us
    all_gather x1 -> x0, waiting for transfers between devices: 29.2 us -> none  [body(): stacked = lax.all_gather(stacked, 'x', axis=2, tiled=True)]
    all_to_all x0 -> x1, waiting for transfers between devices: none -> 8.61 us  [body(): lax.all_to_all(jnp.stack([stacked] * lax.axis_size('x')), 'x', 0, 0)]
    all_gather x1, waiting for transfers between devices: 76.9 us -> 68.8 us  [body(): group_grad = lax.all_gather(group_grad, 'zh', axis=0, tiled=True)]
where the time goes in v1:
time: 464 us
  waiting for transfers between devices  401 us (86%)
  between operations  14.1 us (3%)
  blocking collectives  13.9 us (3%)
  matrix products  11.9 us (3%)
  starting transfers between devices  11.3 us (2%)
  local copies, waits for them, and re-layouts  10.1 us (2%)
    all_gather x1, waiting for transfers between devices, body(): stacked = lax.all_gather(stacked, 'zl', axis=2, tiled=True)  231 us
    all_to_all x1, waiting for transfers between devices, body(): lax.all_to_all(group_grad, DP, split_axis=1, concat_axis=0, tiled=True)  92.7 us
    all_gather x1, waiting for transfers between devices, body(): group_grad = lax.all_gather(group_grad, 'zh', axis=0, tiled=True)  68.8 us
    all_gather x1, blocking collectives, body(): group_grad = lax.all_gather(group_grad, 'y', axis=0, tiled=True)  11.4 us
  transfers between devices with their start and end apart: 4, of which 4 were waited for; matrix products, arithmetic and copies ran while one was open for 1% of the time, Pallas kernels for 0%

profile of v1, /device:TPU:105, one launch (start us, length us, event | category | flops | bytes accessed | tf_op | source)
XLA Modules:
  0.0 463.6 jit_solution(8240255189773664259)
XLA Ops:
  7.2 0.0 copy-start.1
  7.2 1.1 copy.28
  8.3 1.1 copy.29
  9.4 0.1 fusion.15
  9.6 1.0 pad_maximum_fusion
  10.6 0.3 copy.30
  10.8 1.5 stack.19
  12.3 0.0 copy-start.2
  12.3 4.1 all-to-all-start
  16.5 0.0 all-gather.5.cloned.1.call-start
  16.5 0.0 copy-done.1
  16.5 2.5 all_gather.13
  19.0 11.4 %all_gather.14 = bf16[64,4096]{1,0:T(8,128)(2,1)} all-gather(bf16[16,4096]{1,0:T(8,128)(2,1)S(1)} %all_gather.13), channel_id=1, replica_groups=mesh['zl'=8,'x'=4,'zh'=2,'y'=4,'c'=2] {'y'}, dimensions={0}, use_global_device_ids=true | all-gather | bytes 655360 | tf_op jit(solution)/shard_map/all_gather | solution.py:22
  30.4 0.0 all-gather.5.cloned.1.call-update
  30.4 0.0 all-gather.3.cloned.1.call-start
  30.5 8.6 %all-to-all-done = bf16[4,2,896,128]{2,3,1,0:T(8,128)(2,1)S(1)} async-done(((bf16[4,2,896,128]{2,3,1,0:T(8,128)(2,1)}), bf16[4,2,896,128]{2,3,1,0:T(8,128)(2,1)S(1)}, u32[]{:S(2)}, u32[]{:S(2)}) %all-to-all-start) | async-done | bytes 1835040 | tf_op jit(solution)/shard_map/all_to_all | solution.py:32
  39.1 1.4 copy.31
  40.5 0.0 all-gather.3.cloned.1.call-update
  40.6 68.8 %all-gather.5.cloned.1.call-done = bf16[128,4096]{1,0:T(8,128)(2,1)} async-done(((bf16[64,4096]{1,0:T(8,128)(2,1)}), bf16[128,4096]{1,0:T(8,128)(2,1)}) %all-gather.5.cloned.1.call-update) | async-done | bytes 1048592 | tf_op jit(solution)/shard_map/all_gather | solution.py:23
  109.3 2.3 copy.32
  111.6 7.1 %all-to-all-start.1 = ((bf16[128,32,128]{0,2,1:T(8,128)(2,1)}), bf16[128,32,128]{0,2,1:T(8,128)(2,1)S(1)}, u32[]{:S(2)}, u32[]{:S(2)}) async-start(bf16[128,32,128]{0,2,1:T(8,128)(2,1)} %bitcast.8), calls=%async_computation.1 | async-start | bytes 2097152 | tf_op jit(solution)/shard_map/all_to_all | solution.py:29
  118.8 0.0 copy-done.2
  118.8 92.7 %all-to-all-done.1 = bf16[128,32,128]{0,2,1:T(8,128)(2,1)S(1)} async-done(((bf16[128,32,128]{0,2,1:T(8,128)(2,1)}), bf16[128,32,128]{0,2,1:T(8,128)(2,1)S(1)}, u32[]{:S(2)}, u32[]{:S(2)}) %all-to-all-start.1) | async-done | bytes 1048608 | tf_op jit(solution)/shard_map/all_to_all | solution.py:29
  211.5 0.7 copy.33
  212.2 0.0 copy-start
  212.2 0.0 copy-start.3
  212.2 0.0 copy-start.4
  212.2 231.0 %all-gather.3.cloned.1.call-done = bf16[2,896,4096]{1,2,0:T(8,128)(2,1)} async-done(((bf16[2,896,512]{1,2,0:T(8,128)(2,1)}), bf16[2,896,4096]{1,2,0:T(8,128)(2,1)}) %all-gather.3.cloned.1.call-update) | async-done | bytes 14680080 | tf_op jit(solution)/shard_map/all_gather | solution.py:34
  443.2 5.4 %multiply_convert_fusion = (bf16[128,896]{0,1:T(8,128)(2,1)S(1)}, bf16[128,896]{0,1:T(8,128)(2,1)S(1)}) fusion(bf16[128,896]{0,1:T(8,128)(2,1)S(1)} %copy.28, bf16[128,896]{0,1:T(8,128)(2,1)S(1)} %copy.29, bf16[128,4096]{1,0:T(8,128)(2,1)} %all-gather.5.cloned.1.call-done, bf16[2,896,4096]{1,2,0:T(8,128)(2,1)} %all-gather.3.cloned.1.call-done), kind=kOutput, calls=%fused_computation.27 | convolution fusion | flops 941359104 | bytes 9306112 | tf_op jit(solution)/shard_map/dot_general | solution.py:35
  448.7 0.8 copy.34
  449.5 0.8 copy.35
  450.4 0.0 copy-done
  450.4 0.0 copy-done.3
  450.4 0.0 copy-done.4
  450.4 6.4 %fusion.10 = (bf16[896,128]{1,0:T(8,128)(2,1)}, f32[896,128]{1,0:T(8,128)}, f32[896,128]{1,0:T(8,128)}) fusion(bf16[896,128]{1,0:T(8,128)(2,1)S(1)} %copy-done, f32[896]{0:T(1024)S(1)} %convert_multiply_fusion.5, f32[896,128]{1,0:T(8,128)S(1)} %copy-done.3, f32[896,128]{1,0:T(8,128)S(1)} %copy-done.4, bf16[4096,128]{1,0:T(8,128)(2,1)S(1)} %bitcast.31, ...), kind=kOutput, calls=%fused_computation.19 | convolution fusion | flops 941588480 | bytes 10685952 | tf_op jit(solution)/shard_map/dot_general | solution.py:38
  (1 shorter events, 0.0 us)
Async XLA Ops:
  7.2 9.3 %copy-start.1 = (bf16[8,4096]{1,0:T(8,128)(2,1)S(1)}, bf16[8,4096]{1,0:T(8,128)(2,1)}, u32[]{:S(2)}) copy-start(bf16[8,4096]{1,0:T(8,128)(2,1)} %param.7) | copy-start | bytes 196612
  12.3 106.4 %copy-start.2 = (s32[896]{0:T(1024)S(1)}, s32[896]{0:T(1024)}, u32[]{:S(2)}) copy-start(s32[896]{0:T(1024)} %param.13) | copy-start | bytes 10756
  12.3 26.8 %all-to-all-start = ((bf16[4,2,896,128]{2,3,1,0:T(8,128)(2,1)}), bf16[4,2,896,128]{2,3,1,0:T(8,128)(2,1)S(1)}, u32[]{:S(2)}, u32[]{:S(2)}) async-start(bf16[4,2,896,128]{2,3,1,0:T(8,128)(2,1)} %stack.19), calls=%async_computation | async-start | bytes 3670016 | tf_op jit(solution)/shard_map/all_to_all | solution.py:32
  16.5 92.9 %all-gather.5.cloned.1.call-start = ((), (), s32[]{:S(2)}) async-start(), calls=%async_computation.3 | async-start | bytes 1572864 | tf_op jit(solution)/shard_map/all_gather | solution.py:23
  30.4 412.8 %all-gather.3.cloned.1.call-start = ((), (), s32[]{:S(2)}) async-start(), calls=%async_computation.2 | async-start | bytes 16515072 | tf_op jit(solution)/shard_map/all_gather | solution.py:34
  111.6 99.9 %all-to-all-start.1 = ((bf16[128,32,128]{0,2,1:T(8,128)(2,1)}), bf16[128,32,128]{0,2,1:T(8,128)(2,1)S(1)}, u32[]{:S(2)}, u32[]{:S(2)}) async-start(bf16[128,32,128]{0,2,1:T(8,128)(2,1)} %bitcast.8), calls=%async_computation.1 | async-start | bytes 2097152 | tf_op jit(solution)/shard_map/all_to_all | solution.py:29
  212.2 238.2 %copy-start = (bf16[896,128]{1,0:T(8,128)(2,1)S(1)}, bf16[896,128]{1,0:T(8,128)(2,1)}, u32[]{:S(2)}) copy-start(bf16[896,128]{1,0:T(8,128)(2,1)} %param.10) | copy-start | bytes 688132
  212.2 238.2 %copy-start.3 = (f32[896,128]{1,0:T(8,128)S(1)}, f32[896,128]{1,0:T(8,128)}, u32[]{:S(2)}) copy-start(f32[896,128]{1,0:T(8,128)} %param.11) | copy-start | bytes 1376260
  212.2 238.2 %copy-start.4 = (f32[896,128]{1,0:T(8,128)S(1)}, f32[896,128]{1,0:T(8,128)}, u32[]{:S(2)}) copy-start(f32[896,128]{1,0:T(8,128)} %param.12) | copy-start | bytes 1376260
Sparse Core Ops, SparseCore 0:
  30.6 78.7 all-gather.4
  111.4 331.7 all-gather.2
